TPU v7x, 128 devices: a whole 4x4x4 slice. The times are simulated.
128 devices in a mesh: ublk: 16 (over x, z), salt: 8 (over y, core).
Axes of the slice: x: 4, y: 4, z: 4, core: 2. Of those that a mesh axis runs over, the one named last changes fastest.
Arguments:
- user_factors: bfloat16 [16, 8192, 256], P('ublk', 'salt')
- tile_users: int32 [16, 8, 4096], P('ublk', 'salt'), may hold values from 0 to 8191
- tile_items: int32 [16, 8, 4096], P('ublk', 'salt'), may hold values from 0 to 511
- tile_weight: float32 [16, 8, 4096], P('ublk', 'salt'), may hold values from 0.5 to 8
- live_count: int32 [16, 8], P('ublk', 'salt'), may hold values from 2048 to 4096, as said below
Outputs:
- item_factors: float32 [8, 512, 256], P('salt', 'ublk')
- residual: float32 [8, 512, 256], P('salt', 'ublk')
Inputs may be any that keep to these rules, and one draw needn't show every extreme that they name: Every entry of live_count is at least 2048 and at most 4096; some tile is full.
All inputs are finite; a program needn't handle non-finite values.
Results may differ from a plain program's by a relative error of at most 0.0022.
Values may be sent and summed in bfloat16 or wider, within the bound.
A program may use at most 64 MiB of HBM per device.

v0:
```python
import jax
import jax.numpy as jnp
from jax import lax
from jax.sharding import PartitionSpec as P

ITERS = 8
ITEM_DEV = 32
REG = 1.0
EPS = 1e-06


def conjugate(rhs, image_of):
    solution = jnp.zeros_like(rhs)
    resid = rhs
    direction = rhs
    norm_now = jnp.sum(resid * resid, axis=1)
    for step in range(ITERS):
        image = image_of(direction)
        alpha = norm_now / (jnp.sum(direction * image, axis=1) + EPS)
        solution = solution + alpha[:, None] * direction
        resid = resid - alpha[:, None] * image
        norm_next = jnp.sum(resid * resid, axis=1)
        direction = resid + (norm_next / (norm_now + EPS))[:, None] * direction
        norm_now = norm_next
    return (solution, resid)


def body(user_factors, tile_users, tile_items, tile_weight, live_count):
    shard = user_factors[0]
    block = lax.all_gather(shard, "salt", axis=0, tiled=True)
    contract = (((0,), (0,)), ((), ()))
    own_gram = lax.dot_general(shard, shard, contract, preferred_element_type=jnp.float32)
    gram = lax.psum(own_gram, ("ublk", "salt"))
    users = tile_users[0, 0]
    items = tile_items[0, 0]
    raw = tile_weight[0, 0]
    live = jnp.arange(users.shape[0], dtype=jnp.int32) < live_count[0, 0]
    weight = jnp.where(live, raw, jnp.zeros_like(raw))
    confid = jnp.where(live, 1.0 + raw, jnp.zeros_like(raw))
    rows = jnp.take(block, users, axis=0).astype(jnp.float32)
    column_items = ITEM_DEV * lax.axis_size("ublk")
    rhs_terms = jax.ops.segment_sum(confid[:, None] * rows, items, num_segments=column_items)

    def local_terms(whole_dir):
        along = jnp.sum(rows * whole_dir[items], axis=1) * weight
        return jax.ops.segment_sum(along[:, None] * rows, items, num_segments=column_items)

    def finish(summed, direction):
        return summed + jnp.dot(direction, gram, precision=lax.Precision.HIGHEST) + REG * direction

    rhs = lax.psum(rhs_terms, "ublk")

    def image_every(direction):
        summed = lax.psum(local_terms(direction), "ublk")
        return finish(summed, direction)

    solution_all, resid_all = conjugate(rhs, image_every)
    start = lax.axis_index("ublk") * ITEM_DEV
    solution = lax.dynamic_slice_in_dim(solution_all, start, ITEM_DEV, 0)
    resid = lax.dynamic_slice_in_dim(resid_all, start, ITEM_DEV, 0)
    return (solution[None], resid[None])


def solution(mesh):
    return jax.shard_map(
        body,
        mesh=mesh,
        in_specs=(
            P("ublk", "salt", None),
            P("ublk", "salt", None),
            P("ublk", "salt", None),
            P("ublk", "salt", None),
            P("ublk", "salt"),
        ),
        out_specs=(P("salt", "ublk", None), P("salt", "ublk", None)),
        check_vma=False,
    )
```

profile of v0, /device:TPU:0, one launch (start us, length us, event | category | flops | bytes accessed | tf_op | source)
XLA Modules:
  0.0 1352.9 jit_solution(7503660293953594438)
XLA Ops:
  7.2 0.7 all-gather.3.cloned.1.call-update
  8.6 0.7 compare_and_fusion
  9.3 0.7 compare_select_fusion.1
  10.1 0.7 add_select_fusion
  10.8 33.5 %all-gather.3.cloned.1.call-done = bf16[1,8192,256]{2,1,0:T(8,128)(2,1)} async-done(((bf16[1,1024,256]{2,1,0:T(8,128)(2,1)}), bf16[1,8192,256]{2,1,0:T(8,128)(2,1)}) %all-gather.3.cloned.1.call-update) | async-done | bytes 4194320 | tf_op jit(solution)/shard_map/all_gather | solution.py:30
  44.3 15.8 %gather_fusion = bf16[4096,256]{1,0:T(8,128)(2,1)S(1)} fusion(bf16[8192,256]{1,0:T(8,128)(2,1)} %bitcast.43, s32[4096]{0:T(1024)S(1)} %broadcast_clamp_fusion.1), kind=kCustom, calls=%fused_computation | custom fusion | bytes 4210688 | tf_op jit(solution)/shard_map/jit(_take)/gather | solution.py:40
  60.1 26.1 %scatter_custom_fusion = f32[512,256]{1,0:T(8,128)} fusion(s32[4096]{0:T(1024)S(1)} %bitcast.56, f32[4096]{0:T(1024)S(1)} %add_select_fusion, f32[]{:T(128)} %constant.11.clone.1, bf16[4096,256]{1,0:T(8,128)(2,1)S(1)} %gather_fusion, pred[4096]{0:T(1024)(128)(4,1)S(1)} %compare_and_fusion), kind=kCustom, calls=%fused_computation.35 | custom fusion | flops 4194304 | bytes 2641924 | tf_op jit(solution)/shard_map/scatter-add | solution.py:42
  86.3 1.1 fusion.34
  87.4 84.7 %all-reduce.11.cloned.1.call-done = f32[512,256]{1,0:T(8,128)} async-done(((f32[512,256]{1,0:T(8,128)}), f32[512,256]{1,0:T(8,128)}) %all-reduce.11.cloned.1.call-update) | async-done | bytes 524304 | tf_op jit(solution)/shard_map/psum | solution.py:51
  172.1 17.1 %gather_fusion.1 = f32[4096,256]{1,0:T(8,128)} fusion(f32[512,256]{1,0:T(8,128)} %all-reduce.11.cloned.1.call-done, s32[4096]{0:T(1024)S(1)} %broadcast_clamp_fusion), kind=kCustom, calls=%fused_computation.1 | custom fusion | bytes 8404992 | tf_op jit(solution)/shard_map/gather | solution.py:45
  189.2 3.0 fusion.1
  192.2 26.1 %scatter_custom_fusion.1 = f32[512,256]{1,0:T(8,128)} fusion(s32[4096]{0:T(1024)S(1)} %bitcast.57, f32[4096]{0:T(1024)S(1)} %fusion.60, f32[]{:T(128)} %constant.11.clone.1, bf16[4096,256]{1,0:T(8,128)(2,1)S(1)} %gather_fusion, pred[4096]{0:T(1024)(128)(4,1)S(1)} %compare_and_fusion), kind=kCustom, calls=%fused_computation.37 | custom fusion | flops 4194304 | bytes 2641924 | tf_op jit(solution)/shard_map/scatter-add | solution.py:46
  218.4 0.3 all-reduce.17.cloned.1.call-start
  218.7 100.7 %all-reduce.15.cloned.1.call-done = f32[256,256]{1,0:T(8,128)} async-done(((f32[256,256]{1,0:T(8,128)}), f32[256,256]{1,0:T(8,128)}) %all-reduce.15.cloned.1.call-update) | async-done | bytes 262160 | tf_op jit(solution)/shard_map/psum | solution.py:33
  319.4 86.2 %all-reduce.13.cloned.1.call-done = f32[512,256]{1,0:T(8,128)} async-done(((f32[512,256]{1,0:T(8,128)}), f32[512,256]{1,0:T(8,128)}) %all-reduce.13.cloned.1.call-update) | async-done | bytes 524304 | tf_op jit(solution)/shard_map/psum | solution.py:54
  405.6 1.8 multiply_reduce_fusion.14
  407.4 0.2 multiply_reduce_fusion.13
  407.7 0.6 copy-done.4
  408.4 16.1 %gather_fusion.2 = f32[4096,256]{1,0:T(8,128)} fusion(f32[512,256]{1,0:T(8,128)S(1)} %multiply_add_fusion.7, s32[4096]{0:T(1024)S(1)} %broadcast_clamp_fusion), kind=kCustom, calls=%fused_computation.2 | custom fusion | bytes 8404992 | tf_op jit(solution)/shard_map/gather | solution.py:45
  424.5 3.0 fusion.3
  427.5 26.1 %scatter_custom_fusion.2 = f32[512,256]{1,0:T(8,128)} fusion(s32[4096]{0:T(1024)S(1)} %bitcast.58, f32[4096]{0:T(1024)S(1)} %fusion.59, f32[]{:T(128)} %constant.11.clone.1, bf16[4096,256]{1,0:T(8,128)(2,1)S(1)} %gather_fusion, pred[4096]{0:T(1024)(128)(4,1)S(1)} %compare_and_fusion), kind=kCustom, calls=%fused_computation.39 | custom fusion | flops 4194304 | bytes 2641924 | tf_op jit(solution)/shard_map/scatter-add | solution.py:46
  453.7 85.3 %all-reduce.17.cloned.1.call-done = f32[512,256]{1,0:T(8,128)} async-done(((f32[512,256]{1,0:T(8,128)}), f32[512,256]{1,0:T(8,128)}) %all-reduce.17.cloned.1.call-update) | async-done | bytes 524304 | tf_op jit(solution)/shard_map/psum | solution.py:54
  539.0 1.7 multiply_reduce_fusion.12
  540.7 2.1 multiply_reduce_fusion.11
  542.9 16.1 %gather_fusion.3 = f32[4096,256]{1,0:T(8,128)} fusion(f32[512,256]{1,0:T(8,128)S(1)} %multiply_add_fusion.5, s32[4096]{0:T(1024)S(1)} %broadcast_clamp_fusion), kind=kCustom, calls=%fused_computation.3 | custom fusion | bytes 8404992 | tf_op jit(solution)/shard_map/gather | solution.py:45
  559.0 3.5 fusion.5
  562.5 26.5 %scatter_custom_fusion.3 = f32[512,256]{1,0:T(8,128)} fusion(s32[4096]{0:T(1024)S(1)} %bitcast.59, f32[4096]{0:T(1024)S(1)} %fusion.58, f32[]{:T(128)} %constant.11.clone.1, bf16[4096,256]{1,0:T(8,128)(2,1)} %copy-done.1, pred[4096]{0:T(1024)(128)(4,1)S(1)} %compare_and_fusion), kind=kCustom, calls=%fused_computation.41 | custom fusion | flops 4194304 | bytes 2641924 | tf_op jit(solution)/shard_map/scatter-add | solution.py:46
  589.0 0.6 all-reduce.21.cloned.1.call-start
  589.6 84.6 %all-reduce.19.cloned.1.call-done = f32[512,256]{1,0:T(8,128)} async-done(((f32[512,256]{1,0:T(8,128)}), f32[512,256]{1,0:T(8,128)}) %all-reduce.19.cloned.1.call-update) | async-done | bytes 524304 | tf_op jit(solution)/shard_map/psum | solution.py:54
  674.3 1.7 multiply_reduce_fusion.10
  676.0 0.2 multiply_reduce_fusion.9
  676.2 1.0 broadcast_multiply_fusion
  677.3 16.1 %gather_fusion.4 = f32[4096,256]{1,0:T(8,128)} fusion(f32[512,256]{1,0:T(8,128)S(1)} %get-tuple-element.18, s32[4096]{0:T(1024)S(1)} %broadcast_clamp_fusion), kind=kCustom, calls=%fused_computation.4 | custom fusion | bytes 8404992 | tf_op jit(solution)/shard_map/gather | solution.py:45
  693.3 3.0 fusion.7
  696.4 26.1 %scatter_custom_fusion.4 = f32[512,256]{1,0:T(8,128)} fusion(s32[4096]{0:T(1024)S(1)} %bitcast.60, f32[4096]{0:T(1024)S(1)} %fusion.57, f32[]{:T(128)} %constant.11.clone.1, bf16[4096,256]{1,0:T(8,128)(2,1)S(1)} %copy-done.2, pred[4096]{0:T(1024)(128)(4,1)S(1)} %compare_and_fusion), kind=kCustom, calls=%fused_computation.43 | custom fusion | flops 4194304 | bytes 2641924 | tf_op jit(solution)/shard_map/scatter-add | solution.py:46
  722.6 85.2 %all-reduce.21.cloned.1.call-done = f32[512,256]{1,0:T(8,128)} async-done(((f32[512,256]{1,0:T(8,128)}), f32[512,256]{1,0:T(8,128)}) %all-reduce.21.cloned.1.call-update) | async-done | bytes 524304 | tf_op jit(solution)/shard_map/psum | solution.py:54
  807.8 1.7 multiply_reduce_fusion.8
  809.5 0.2 multiply_reduce_fusion.7
  809.8 0.8 copy-done.5
  810.7 16.1 %gather_fusion.5 = f32[4096,256]{1,0:T(8,128)} fusion(f32[512,256]{1,0:T(8,128)S(1)} %multiply_add_fusion.3, s32[4096]{0:T(1024)S(1)} %broadcast_clamp_fusion), kind=kCustom, calls=%fused_computation.5 | custom fusion | bytes 8404992 | tf_op jit(solution)/shard_map/gather | solution.py:45
  826.8 2.9 fusion.9
  829.7 26.1 %scatter_custom_fusion.5 = f32[512,256]{1,0:T(8,128)} fusion(s32[4096]{0:T(1024)S(1)} %bitcast.61, f32[4096]{0:T(1024)S(1)} %fusion.56, f32[]{:T(128)} %constant.11.clone.1, bf16[4096,256]{1,0:T(8,128)(2,1)S(1)} %copy-done.2, pred[4096]{0:T(1024)(128)(4,1)S(1)} %compare_and_fusion), kind=kCustom, calls=%fused_computation.45 | custom fusion | flops 4194304 | bytes 2641924 | tf_op jit(solution)/shard_map/scatter-add | solution.py:46
  856.1 85.1 %all-reduce.23.cloned.1.call-done = f32[512,256]{1,0:T(8,128)} async-done(((f32[512,256]{1,0:T(8,128)}), f32[512,256]{1,0:T(8,128)}) %all-reduce.23.cloned.1.call-update) | async-done | bytes 524304 | tf_op jit(solution)/shard_map/psum | solution.py:54
  941.2 1.7 multiply_reduce_fusion.6
  942.9 1.3 multiply_reduce_fusion.5
  944.4 16.1 %gather_fusion.6 = f32[4096,256]{1,0:T(8,128)} fusion(f32[512,256]{1,0:T(8,128)S(1)} %multiply_add_fusion.2, s32[4096]{0:T(1024)S(1)} %broadcast_clamp_fusion), kind=kCustom, calls=%fused_computation.6 | custom fusion | bytes 8404992 | tf_op jit(solution)/shard_map/gather | solution.py:45
  960.4 3.5 fusion.11
  963.9 26.5 %scatter_custom_fusion.6 = f32[512,256]{1,0:T(8,128)} fusion(s32[4096]{0:T(1024)S(1)} %bitcast.62, f32[4096]{0:T(1024)S(1)} %fusion.55, f32[]{:T(128)} %constant.11.clone.1, bf16[4096,256]{1,0:T(8,128)(2,1)} %copy-done.1, pred[4096]{0:T(1024)(128)(4,1)S(1)} %compare_and_fusion), kind=kCustom, calls=%fused_computation.47 | custom fusion | flops 4194304 | bytes 2641924 | tf_op jit(solution)/shard_map/scatter-add | solution.py:46
  990.5 85.2 %all-reduce.25.cloned.1.call-done = f32[512,256]{1,0:T(8,128)} async-done(((f32[512,256]{1,0:T(8,128)}), f32[512,256]{1,0:T(8,128)}) %all-reduce.25.cloned.1.call-update) | async-done | bytes 524304 | tf_op jit(solution)/shard_map/psum | solution.py:54
  1075.8 1.7 multiply_reduce_fusion.4
  1077.5 0.2 multiply_reduce_fusion.3
  1077.9 16.1 %gather_fusion.7 = f32[4096,256]{1,0:T(8,128)} fusion(f32[512,256]{1,0:T(8,128)S(1)} %multiply_add_fusion.1, s32[4096]{0:T(1024)S(1)} %broadcast_clamp_fusion), kind=kCustom, calls=%fused_computation.7 | custom fusion | bytes 8404992 | tf_op jit(solution)/shard_map/gather | solution.py:45
  1094.0 3.5 fusion.13
  1097.5 26.5 %scatter_custom_fusion.7 = f32[512,256]{1,0:T(8,128)} fusion(s32[4096]{0:T(1024)S(1)} %bitcast.63, f32[4096]{0:T(1024)S(1)} %fusion.54, f32[]{:T(128)} %constant.11.clone.1, bf16[4096,256]{1,0:T(8,128)(2,1)} %copy-done.1, pred[4096]{0:T(1024)(128)(4,1)S(1)} %compare_and_fusion), kind=kCustom, calls=%fused_computation.49 | custom fusion | flops 4194304 | bytes 2641924 | tf_op jit(solution)/shard_map/scatter-add | solution.py:46
  1124.0 0.3 all-reduce.29.cloned.1.call-start
  1124.3 85.0 %all-reduce.27.cloned.1.call-done = f32[512,256]{1,0:T(8,128)} async-done(((f32[512,256]{1,0:T(8,128)}), f32[512,256]{1,0:T(8,128)}) %all-reduce.27.cloned.1.call-update) | async-done | bytes 524304 | tf_op jit(solution)/shard_map/psum | solution.py:54
  1209.3 1.7 multiply_reduce_fusion.2
  1211.0 0.2 multiply_reduce_fusion.1
  1211.4 16.1 %gather_fusion.8 = f32[4096,256]{1,0:T(8,128)} fusion(f32[512,256]{1,0:T(8,128)S(1)} %multiply_add_fusion, s32[4096]{0:T(1024)S(1)} %broadcast_clamp_fusion), kind=kCustom, calls=%fused_computation.8 | custom fusion | bytes 8404992 | tf_op jit(solution)/shard_map/gather | solution.py:45
  1227.5 3.5 fusion.15
  1231.0 26.5 %scatter_custom_fusion.8 = f32[512,256]{1,0:T(8,128)} fusion(s32[4096]{0:T(1024)S(1)} %bitcast.64, f32[4096]{0:T(1024)S(1)} %fusion.53, f32[]{:T(128)} %constant.11.clone.1, bf16[4096,256]{1,0:T(8,128)(2,1)} %copy-done.1, pred[4096]{0:T(1024)(128)(4,1)S(1)} %compare_and_fusion), kind=kCustom, calls=%fused_computation.51 | custom fusion | flops 4194304 | bytes 2641924 | tf_op jit(solution)/shard_map/scatter-add | solution.py:46
  1257.8 85.0 %all-reduce.29.cloned.1.call-done = f32[512,256]{1,0:T(8,128)} async-done(((f32[512,256]{1,0:T(8,128)}), f32[512,256]{1,0:T(8,128)}) %all-reduce.29.cloned.1.call-update) | async-done | bytes 524304 | tf_op jit(solution)/shard_map/psum | solution.py:54
  1342.8 1.7 multiply_reduce_fusion
  1344.6 1.5 fusion.45
  (75 shorter events, 2.2 us)
Async XLA Ops:
  7.2 37.1 %all-gather.3.cloned.1.call-start = ((), (), s32[]{:S(2)}) async-start(), calls=%async_computation.10 | async-start | bytes 4718592 | tf_op jit(solution)/shard_map/all_gather | solution.py:30
  7.9 164.2 %all-reduce.11.cloned.1.call-start = ((), (), s32[]{:S(2)}) async-start(), calls=%async_computation | async-start | bytes 1048576 | tf_op jit(solution)/shard_map/psum | solution.py:51
  44.3 15.8 %copy-start.10 = (s32[1,1,4096]{2,1,0:T(1,128)S(1)}, s32[1,1,4096]{2,1,0:T(1,128)}, u32[]{:S(2)}) copy-start(s32[1,1,4096]{2,1,0:T(1,128)} %param.7) | copy-start | bytes 49156
  44.3 42.0 %copy-start.9 = (bf16[1,1024,256]{2,1,0:T(8,128)(2,1)S(1)}, bf16[1,1024,256]{2,1,0:T(8,128)(2,1)}, u32[]{:S(2)}) copy-start(bf16[1,1024,256]{2,1,0:T(8,128)(2,1)} %param.5) | copy-start | bytes 1572868
  60.1 367.5 %copy-start.1 = (bf16[4096,256]{1,0:T(8,128)(2,1)}, bf16[4096,256]{1,0:T(8,128)(2,1)S(1)}, u32[]{:S(2)}) copy-start(bf16[4096,256]{1,0:T(8,128)(2,1)S(1)} %gather_fusion) | copy-start | bytes 6291460
  86.2 233.2 %all-reduce.15.cloned.1.call-start = ((), (), s32[]{:S(2)}) async-start(), calls=%async_computation.2 | async-start | bytes 524288 | tf_op jit(solution)/shard_map/psum | solution.py:33
  87.3 318.2 %all-reduce.13.cloned.1.call-start = ((), (), s32[]{:S(2)}) async-start(), calls=%async_computation.1 | async-start | bytes 1048576 | tf_op jit(solution)/shard_map/psum | solution.py:54
  189.2 3.0 copy-start.8
  189.2 216.4 %copy-start = (f32[512,256]{1,0:T(8,128)S(1)}, f32[512,256]{1,0:T(8,128)}, u32[]{:S(2)}) copy-start(f32[512,256]{1,0:T(8,128)} %all-reduce.11.cloned.1.call-done) | copy-start | bytes 1572868
  218.4 320.6 %all-reduce.17.cloned.1.call-start = ((), (), s32[]{:S(2)}) async-start(), calls=%async_computation.3 | async-start | bytes 1048576 | tf_op jit(solution)/shard_map/psum | solution.py:54
  407.4 0.8 copy-start.4
  424.5 114.5 %copy-start.3 = (f32[256,256]{1,0:T(8,128)S(1)}, f32[256,256]{1,0:T(8,128)}, u32[]{:S(2)}) copy-start(f32[256,256]{1,0:T(8,128)} %all-reduce.15.cloned.1.call-done) | copy-start | bytes 786436
  453.6 220.6 %all-reduce.19.cloned.1.call-start = ((), (), s32[]{:S(2)}) async-start(), calls=%async_computation.4 | async-start | bytes 1048576 | tf_op jit(solution)/shard_map/psum | solution.py:54
  589.0 218.8 %all-reduce.21.cloned.1.call-start = ((), (), s32[]{:S(2)}) async-start(), calls=%async_computation.5 | async-start | bytes 1048576 | tf_op jit(solution)/shard_map/psum | solution.py:54
  676.2 1.0 copy-start.6
  677.3 16.1 %copy-start.2 = (bf16[4096,256]{1,0:T(8,128)(2,1)S(1)}, bf16[4096,256]{1,0:T(8,128)(2,1)}, u32[]{:S(2)}) copy-start(bf16[4096,256]{1,0:T(8,128)(2,1)} %copy-done.1) | copy-start | bytes 6291460
  693.3 116.2 %copy-start.7 = (f32[512,256]{1,0:T(8,128)S(1)}, f32[512,256]{1,0:T(8,128)}, u32[]{:S(2)}) copy-start(f32[512,256]{1,0:T(8,128)} %copy-done.6) | copy-start | bytes 1572868
  722.5 218.7 %all-reduce.23.cloned.1.call-start = ((), (), s32[]{:S(2)}) async-start(), calls=%async_computation.6 | async-start | bytes 1048576 | tf_op jit(solution)/shard_map/psum | solution.py:54
  809.8 0.8 copy-start.5
  855.9 219.9 %all-reduce.25.cloned.1.call-start = ((), (), s32[]{:S(2)}) async-start(), calls=%async_computation.7 | async-start | bytes 1048576 | tf_op jit(solution)/shard_map/psum | solution.py:54
  990.5 218.8 %all-reduce.27.cloned.1.call-start = ((), (), s32[]{:S(2)}) async-start(), calls=%async_computation.8 | async-start | bytes 1048576 | tf_op jit(solution)/shard_map/psum | solution.py:54
  1124.0 218.8 %all-reduce.29.cloned.1.call-start = ((), (), s32[]{:S(2)}) async-start(), calls=%async_computation.9 | async-start | bytes 1048576 | tf_op jit(solution)/shard_map/psum | solution.py:54
Sparse Core Ops, SparseCore 0:
  9.7 34.5 all-gather.2
  86.3 85.7 all-reduce.10
  176.8 142.5 all-reduce.14
  322.5 83.0 all-reduce.12
  453.8 85.1 all-reduce.16
  589.2 85.0 all-reduce.18
  722.6 85.1 all-reduce.20
  856.0 85.1 all-reduce.22
  990.6 85.1 all-reduce.24
  1124.1 85.1 all-reduce.26
  1257.6 85.1 all-reduce.28
where the time goes:
time: 1360 us; the launch traced here: 1350 us
  waiting for transfers between devices  901 us (66%)
  other arithmetic  273 us (20%)
  local copies, waits for them, and re-layouts  147 us (11%)
  between operations  15.1 us (1%)
  matrix products  14.8 us (1%)
    psum x8, waiting for transfers between devices, image_every(): summed = lax.psum(local_terms(direction), 'ublk')  682 us
    scatter-add x8, other arithmetic, local_terms(): jax.ops.segment_sum(along[:, None] * rows, items, num_segments=column_items)  210 us
    gather x8, local copies, waits for them, and re-layouts, local_terms(): along = jnp.sum(rows * whole_dir[items], axis=1) * weight  130 us
    psum x1, waiting for transfers between devices, body(): gram = lax.psum(own_gram, ('ublk', 'salt'))  101 us
    psum x1, waiting for transfers between devices, body(): rhs = lax.psum(rhs_terms, 'ublk')  84.7 us
    all_gather x1, waiting for transfers between devices, body(): block = lax.all_gather(shard, 'salt', axis=0, tiled=True)  33.5 us
  transfers between devices with their start and end apart: 11, of which 11 were waited for; matrix products, arithmetic and copies ran while one was open for 4% of the time, Pallas kernels for 0%

commit v1 on v0

--- a/solution.py
+++ b/solution.py
@@ -48,7 +48,10 @@
     def finish(summed, direction):
         return summed + jnp.dot(direction, gram, precision=lax.Precision.HIGHEST) + REG * direction
 
-    rhs = lax.psum(rhs_terms, "ublk")
+    size, rhs = (lax.axis_size("ublk"), rhs_terms)
+    for far in [1 << k for k in range(size.bit_length() - 1)]:
+        swap = [(i, i ^ far) for i in range(size)]
+        rhs = rhs + lax.ppermute(rhs, "ublk", swap)
 
     def image_every(direction):
         summed = lax.psum(local_terms(direction), "ublk")

time: 1360 us -> 1300 us (0.956)
  waiting for transfers between devices: 901 us -> 833 us
    psum x1 -> x0, waiting for transfers between devices: 84.7 us -> none  [body(): rhs = lax.psum(rhs_terms, 'ublk')]
    ppermute x0 -> x4, waiting for transfers between devices: none -> 43.1 us  [body(): rhs = rhs + lax.ppermute(rhs, 'ublk', swap)]
    psum x1, waiting for transfers between devices: 101 us -> 78.1 us  [body(): gram = lax.psum(own_gram, ('ublk', 'salt'))]
  transfers between devices with their start and end apart: 11 -> 14, of which waited for: 11 -> 14; matrix products, arithmetic and copies ran while one was open for 4% -> 4% of each run, Pallas kernels for 0% -> 0%
where the time goes in v1:
time: 1300 us
  waiting for transfers between devices  833 us (64%)
  other arithmetic  272 us (21%)
  local copies, waits for them, and re-layouts  146 us (11%)
  between operations  17 us (1%)
  matrix products  16 us (1%)
    psum x8, waiting for transfers between devices, image_every(): summed = lax.psum(local_terms(direction), 'ublk')  678 us
    scatter-add x8, other arithmetic, local_terms(): jax.ops.segment_sum(along[:, None] * rows, items, num_segments=column_items)  210 us
    gather x8, local copies, waits for them, and re-layouts, local_terms(): along = jnp.sum(rows * whole_dir[items], axis=1) * weight  129 us
    psum x1, waiting for transfers between devices, body(): gram = lax.psum(own_gram, ('ublk', 'salt'))  78.1 us
    ppermute x4, waiting for transfers between devices, body(): rhs = rhs + lax.ppermute(rhs, 'ublk', swap)  43.1 us
    all_gather x1, waiting for transfers between devices, body(): block = lax.all_gather(shard, 'salt', axis=0, tiled=True)  33.5 us
  transfers between devices with their start and end apart: 14, of which 14 were waited for; matrix products, arithmetic and copies ran while one was open for 4% of the time, Pallas kernels for 0%

profile of v1, /device:TPU:0, one launch (start us, length us, event | category | flops | bytes accessed | tf_op | source)
XLA Modules:
  0.0 1295.6 jit_solution(15525109093016080871)
XLA Ops:
  8.0 0.7 all-gather.3.cloned.1.call-update
  9.4 0.7 compare_and_fusion
  10.2 0.7 compare_select_fusion.1
  10.9 0.7 add_select_fusion
  11.6 33.5 %all-gather.3.cloned.1.call-done = bf16[1,8192,256]{2,1,0:T(8,128)(2,1)} async-done(((bf16[1,1024,256]{2,1,0:T(8,128)(2,1)}), bf16[1,8192,256]{2,1,0:T(8,128)(2,1)}) %all-gather.3.cloned.1.call-update) | async-done | bytes 4194320 | tf_op jit(solution)/shard_map/all_gather | solution.py:30
  45.1 15.7 %gather_fusion = bf16[4096,256]{1,0:T(8,128)(2,1)S(1)} fusion(bf16[8192,256]{1,0:T(8,128)(2,1)} %bitcast.43, s32[4096]{0:T(1024)S(1)} %broadcast_clamp_fusion.1), kind=kCustom, calls=%fused_computation | custom fusion | bytes 4210688 | tf_op jit(solution)/shard_map/jit(_take)/gather | solution.py:40
  60.9 25.4 %scatter_custom_fusion = f32[512,256]{1,0:T(8,128)S(1)} fusion(s32[4096]{0:T(1024)S(1)} %bitcast.56, f32[4096]{0:T(1024)S(1)} %add_select_fusion, f32[]{:T(128)} %constant.11.clone.1, bf16[4096,256]{1,0:T(8,128)(2,1)S(1)} %gather_fusion, pred[4096]{0:T(1024)(128)(4,1)S(1)} %compare_and_fusion), kind=kCustom, calls=%fused_computation.35 | custom fusion | flops 4194304 | bytes 2641924 | tf_op jit(solution)/shard_map/scatter-add | solution.py:42
  86.3 1.6 collective-permute-start
  88.0 12.5 collective-permute-done
  100.5 3.2 collective-permute-start.1
  103.8 11.6 collective-permute-done.1
  115.4 1.5 collective-permute-start.2
  117.0 2.2 fusion.34
  119.3 8.6 collective-permute-done.2
  127.9 3.1 collective-permute-start.3
  131.0 10.5 collective-permute-done.3
  141.6 16.1 %gather_fusion.1 = f32[4096,256]{1,0:T(8,128)} fusion(f32[512,256]{1,0:T(8,128)S(1)} %add.304, s32[4096]{0:T(1024)S(1)} %broadcast_clamp_fusion), kind=kCustom, calls=%fused_computation.1 | custom fusion | bytes 8404992 | tf_op jit(solution)/shard_map/gather | solution.py:45
  157.7 3.0 fusion.1
  160.7 26.1 %scatter_custom_fusion.1 = f32[512,256]{1,0:T(8,128)} fusion(s32[4096]{0:T(1024)S(1)} %bitcast.57, f32[4096]{0:T(1024)S(1)} %fusion.60, f32[]{:T(128)} %constant.11.clone.1, bf16[4096,256]{1,0:T(8,128)(2,1)S(1)} %gather_fusion, pred[4096]{0:T(1024)(128)(4,1)S(1)} %compare_and_fusion), kind=kCustom, calls=%fused_computation.37 | custom fusion | flops 4194304 | bytes 2641924 | tf_op jit(solution)/shard_map/scatter-add | solution.py:46
  187.1 78.1 %all-reduce.12.cloned.1.call-done = f32[256,256]{1,0:T(8,128)} async-done(((f32[256,256]{1,0:T(8,128)}), f32[256,256]{1,0:T(8,128)}) %all-reduce.12.cloned.1.call-update) | async-done | bytes 262160 | tf_op jit(solution)/shard_map/psum | solution.py:33
  265.3 85.7 %all-reduce.10.cloned.1.call-done = f32[512,256]{1,0:T(8,128)} async-done(((f32[512,256]{1,0:T(8,128)}), f32[512,256]{1,0:T(8,128)}) %all-reduce.10.cloned.1.call-update) | async-done | bytes 524304 | tf_op jit(solution)/shard_map/psum | solution.py:57
  351.0 1.8 multiply_reduce_fusion.14
  353.1 0.6 copy-done.3
  353.9 16.1 %gather_fusion.2 = f32[4096,256]{1,0:T(8,128)} fusion(f32[512,256]{1,0:T(8,128)S(1)} %multiply_add_fusion.7, s32[4096]{0:T(1024)S(1)} %broadcast_clamp_fusion), kind=kCustom, calls=%fused_computation.2 | custom fusion | bytes 8404992 | tf_op jit(solution)/shard_map/gather | solution.py:45
  369.9 3.0 fusion.3
  372.9 26.1 %scatter_custom_fusion.2 = f32[512,256]{1,0:T(8,128)} fusion(s32[4096]{0:T(1024)S(1)} %bitcast.58, f32[4096]{0:T(1024)S(1)} %fusion.59, f32[]{:T(128)} %constant.11.clone.1, bf16[4096,256]{1,0:T(8,128)(2,1)S(1)} %gather_fusion, pred[4096]{0:T(1024)(128)(4,1)S(1)} %compare_and_fusion), kind=kCustom, calls=%fused_computation.39 | custom fusion | flops 4194304 | bytes 2641924 | tf_op jit(solution)/shard_map/scatter-add | solution.py:46
  399.1 84.7 %all-reduce.14.cloned.1.call-done = f32[512,256]{1,0:T(8,128)} async-done(((f32[512,256]{1,0:T(8,128)}), f32[512,256]{1,0:T(8,128)}) %all-reduce.14.cloned.1.call-update) | async-done | bytes 524304 | tf_op jit(solution)/shard_map/psum | solution.py:57
  483.8 1.7 multiply_reduce_fusion.12
  485.6 2.1 multiply_reduce_fusion.11
  487.8 16.1 %gather_fusion.3 = f32[4096,256]{1,0:T(8,128)} fusion(f32[512,256]{1,0:T(8,128)S(1)} %multiply_add_fusion.5, s32[4096]{0:T(1024)S(1)} %broadcast_clamp_fusion), kind=kCustom, calls=%fused_computation.3 | custom fusion | bytes 8404992 | tf_op jit(solution)/shard_map/gather | solution.py:45
  503.9 3.5 fusion.5
  507.4 26.5 %scatter_custom_fusion.3 = f32[512,256]{1,0:T(8,128)} fusion(s32[4096]{0:T(1024)S(1)} %bitcast.59, f32[4096]{0:T(1024)S(1)} %fusion.58, f32[]{:T(128)} %constant.11.clone.1, bf16[4096,256]{1,0:T(8,128)(2,1)} %copy-done, pred[4096]{0:T(1024)(128)(4,1)S(1)} %compare_and_fusion), kind=kCustom, calls=%fused_computation.41 | custom fusion | flops 4194304 | bytes 2641924 | tf_op jit(solution)/shard_map/scatter-add | solution.py:46
  533.9 0.6 all-reduce.18.cloned.1.call-start
  534.5 84.2 %all-reduce.16.cloned.1.call-done = f32[512,256]{1,0:T(8,128)} async-done(((f32[512,256]{1,0:T(8,128)}), f32[512,256]{1,0:T(8,128)}) %all-reduce.16.cloned.1.call-update) | async-done | bytes 524304 | tf_op jit(solution)/shard_map/psum | solution.py:57
  618.7 1.7 multiply_reduce_fusion.10
  620.6 1.0 broadcast_multiply_fusion
  621.7 16.1 %gather_fusion.4 = f32[4096,256]{1,0:T(8,128)} fusion(f32[512,256]{1,0:T(8,128)S(1)} %get-tuple-element.18, s32[4096]{0:T(1024)S(1)} %broadcast_clamp_fusion), kind=kCustom, calls=%fused_computation.4 | custom fusion | bytes 8404992 | tf_op jit(solution)/shard_map/gather | solution.py:45
  637.7 3.0 fusion.7
  640.8 26.1 %scatter_custom_fusion.4 = f32[512,256]{1,0:T(8,128)} fusion(s32[4096]{0:T(1024)S(1)} %bitcast.60, f32[4096]{0:T(1024)S(1)} %fusion.57, f32[]{:T(128)} %constant.11.clone.1, bf16[4096,256]{1,0:T(8,128)(2,1)S(1)} %copy-done.1, pred[4096]{0:T(1024)(128)(4,1)S(1)} %compare_and_fusion), kind=kCustom, calls=%fused_computation.43 | custom fusion | flops 4194304 | bytes 2641924 | tf_op jit(solution)/shard_map/scatter-add | solution.py:46
  667.0 84.7 %all-reduce.18.cloned.1.call-done = f32[512,256]{1,0:T(8,128)} async-done(((f32[512,256]{1,0:T(8,128)}), f32[512,256]{1,0:T(8,128)}) %all-reduce.18.cloned.1.call-update) | async-done | bytes 524304 | tf_op jit(solution)/shard_map/psum | solution.py:57
  751.7 1.7 multiply_reduce_fusion.8
  753.7 0.8 copy-done.4
  754.6 16.1 %gather_fusion.5 = f32[4096,256]{1,0:T(8,128)} fusion(f32[512,256]{1,0:T(8,128)S(1)} %multiply_add_fusion.3, s32[4096]{0:T(1024)S(1)} %broadcast_clamp_fusion), kind=kCustom, calls=%fused_computation.5 | custom fusion | bytes 8404992 | tf_op jit(solution)/shard_map/gather | solution.py:45
  770.6 2.9 fusion.9
  773.6 26.1 %scatter_custom_fusion.5 = f32[512,256]{1,0:T(8,128)} fusion(s32[4096]{0:T(1024)S(1)} %bitcast.61, f32[4096]{0:T(1024)S(1)} %fusion.56, f32[]{:T(128)} %constant.11.clone.1, bf16[4096,256]{1,0:T(8,128)(2,1)S(1)} %copy-done.1, pred[4096]{0:T(1024)(128)(4,1)S(1)} %compare_and_fusion), kind=kCustom, calls=%fused_computation.45 | custom fusion | flops 4194304 | bytes 2641924 | tf_op jit(solution)/shard_map/scatter-add | solution.py:46
  800.0 84.5 %all-reduce.20.cloned.1.call-done = f32[512,256]{1,0:T(8,128)} async-done(((f32[512,256]{1,0:T(8,128)}), f32[512,256]{1,0:T(8,128)}) %all-reduce.20.cloned.1.call-update) | async-done | bytes 524304 | tf_op jit(solution)/shard_map/psum | solution.py:57
  884.5 1.7 multiply_reduce_fusion.6
  886.2 1.3 multiply_reduce_fusion.5
  887.6 16.1 %gather_fusion.6 = f32[4096,256]{1,0:T(8,128)} fusion(f32[512,256]{1,0:T(8,128)S(1)} %multiply_add_fusion.2, s32[4096]{0:T(1024)S(1)} %broadcast_clamp_fusion), kind=kCustom, calls=%fused_computation.6 | custom fusion | bytes 8404992 | tf_op jit(solution)/shard_map/gather | solution.py:45
  903.7 3.5 fusion.11
  907.2 26.5 %scatter_custom_fusion.6 = f32[512,256]{1,0:T(8,128)} fusion(s32[4096]{0:T(1024)S(1)} %bitcast.62, f32[4096]{0:T(1024)S(1)} %fusion.55, f32[]{:T(128)} %constant.11.clone.1, bf16[4096,256]{1,0:T(8,128)(2,1)} %copy-done, pred[4096]{0:T(1024)(128)(4,1)S(1)} %compare_and_fusion), kind=kCustom, calls=%fused_computation.47 | custom fusion | flops 4194304 | bytes 2641924 | tf_op jit(solution)/shard_map/scatter-add | solution.py:46
  933.8 84.7 %all-reduce.22.cloned.1.call-done = f32[512,256]{1,0:T(8,128)} async-done(((f32[512,256]{1,0:T(8,128)}), f32[512,256]{1,0:T(8,128)}) %all-reduce.22.cloned.1.call-update) | async-done | bytes 524304 | tf_op jit(solution)/shard_map/psum | solution.py:57
  1018.5 1.7 multiply_reduce_fusion.4
  1020.7 16.1 %gather_fusion.7 = f32[4096,256]{1,0:T(8,128)} fusion(f32[512,256]{1,0:T(8,128)S(1)} %multiply_add_fusion.1, s32[4096]{0:T(1024)S(1)} %broadcast_clamp_fusion), kind=kCustom, calls=%fused_computation.7 | custom fusion | bytes 8404992 | tf_op jit(solution)/shard_map/gather | solution.py:45
  1036.7 3.5 fusion.13
  1040.2 26.5 %scatter_custom_fusion.7 = f32[512,256]{1,0:T(8,128)} fusion(s32[4096]{0:T(1024)S(1)} %bitcast.63, f32[4096]{0:T(1024)S(1)} %fusion.54, f32[]{:T(128)} %constant.11.clone.1, bf16[4096,256]{1,0:T(8,128)(2,1)} %copy-done, pred[4096]{0:T(1024)(128)(4,1)S(1)} %compare_and_fusion), kind=kCustom, calls=%fused_computation.49 | custom fusion | flops 4194304 | bytes 2641924 | tf_op jit(solution)/shard_map/scatter-add | solution.py:46
  1067.0 84.5 %all-reduce.24.cloned.1.call-done = f32[512,256]{1,0:T(8,128)} async-done(((f32[512,256]{1,0:T(8,128)}), f32[512,256]{1,0:T(8,128)}) %all-reduce.24.cloned.1.call-update) | async-done | bytes 524304 | tf_op jit(solution)/shard_map/psum | solution.py:57
  1151.6 1.7 multiply_reduce_fusion.2
  1153.7 16.1 %gather_fusion.8 = f32[4096,256]{1,0:T(8,128)} fusion(f32[512,256]{1,0:T(8,128)S(1)} %multiply_add_fusion, s32[4096]{0:T(1024)S(1)} %broadcast_clamp_fusion), kind=kCustom, calls=%fused_computation.8 | custom fusion | bytes 8404992 | tf_op jit(solution)/shard_map/gather | solution.py:45
  1169.7 3.5 fusion.15
  1173.2 26.5 %scatter_custom_fusion.8 = f32[512,256]{1,0:T(8,128)} fusion(s32[4096]{0:T(1024)S(1)} %bitcast.64, f32[4096]{0:T(1024)S(1)} %fusion.53, f32[]{:T(128)} %constant.11.clone.1, bf16[4096,256]{1,0:T(8,128)(2,1)} %copy-done, pred[4096]{0:T(1024)(128)(4,1)S(1)} %compare_and_fusion), kind=kCustom, calls=%fused_computation.51 | custom fusion | flops 4194304 | bytes 2641924 | tf_op jit(solution)/shard_map/scatter-add | solution.py:46
  1200.1 84.5 %all-reduce.26.cloned.1.call-done = f32[512,256]{1,0:T(8,128)} async-done(((f32[512,256]{1,0:T(8,128)}), f32[512,256]{1,0:T(8,128)}) %all-reduce.26.cloned.1.call-update) | async-done | bytes 524304 | tf_op jit(solution)/shard_map/psum | solution.py:57
  1284.5 1.7 multiply_reduce_fusion
  1286.3 1.5 fusion.45
  (80 shorter events, 4.2 us)
Async XLA Ops:
  8.0 37.1 %all-gather.3.cloned.1.call-start = ((), (), s32[]{:S(2)}) async-start(), calls=%async_computation.9 | async-start | bytes 4718592 | tf_op jit(solution)/shard_map/all_gather | solution.py:30
  8.7 256.5 %all-reduce.12.cloned.1.call-start = ((), (), s32[]{:S(2)}) async-start(), calls=%async_computation.1 | async-start | bytes 524288 | tf_op jit(solution)/shard_map/psum | solution.py:33
  45.1 15.8 %copy-start.8 = (s32[1,1,4096]{2,1,0:T(1,128)S(1)}, s32[1,1,4096]{2,1,0:T(1,128)}, u32[]{:S(2)}) copy-start(s32[1,1,4096]{2,1,0:T(1,128)} %param.7) | copy-start | bytes 49156
  60.8 312.1 %copy-start = (bf16[4096,256]{1,0:T(8,128)(2,1)}, bf16[4096,256]{1,0:T(8,128)(2,1)S(1)}, u32[]{:S(2)}) copy-start(bf16[4096,256]{1,0:T(8,128)(2,1)S(1)} %gather_fusion) | copy-start | bytes 6291460
  86.3 14.1 %collective-permute-start = (f32[512,256]{1,0:T(8,128)S(1)}, f32[512,256]{1,0:T(8,128)S(1)}, u32[]{:S(2)}, u32[]{:S(2)}) collective-permute-start(f32[512,256]{1,0:T(8,128)S(1)} %scatter_custom_fusion), channel_id=1, source_target_pairs={{0,8},{8,0},{16,24},{24,16},{32,40},{40,32},{48,56},{56,48},{64,72... | collective-permute-start | bytes 1572872 | tf_op jit(solution)/shard_map/ppermute | solution.py:54
  100.5 14.8 %collective-permute-start.1 = (f32[512,256]{1,0:T(8,128)S(1)}, f32[512,256]{1,0:T(8,128)S(1)}, u32[]{:S(2)}, u32[]{:S(2)}) collective-permute-start(f32[512,256]{1,0:T(8,128)S(1)} %add.301), channel_id=1, source_target_pairs={{0,16},{8,24},{16,0},{24,8},{32,48},{40,56},{48,32},{56,40},{64,80... | collective-permute-start | bytes 1572872 | tf_op jit(solution)/shard_map/ppermute | solution.py:54
  115.4 12.4 collective-permute-start.2
  119.2 231.8 %all-reduce.10.cloned.1.call-start = ((), (), s32[]{:S(2)}) async-start(), calls=%async_computation | async-start | bytes 1048576 | tf_op jit(solution)/shard_map/psum | solution.py:57
  127.9 13.6 %collective-permute-start.3 = (f32[512,256]{1,0:T(8,128)S(1)}, f32[512,256]{1,0:T(8,128)S(1)}, u32[]{:S(2)}, u32[]{:S(2)}) collective-permute-start(f32[512,256]{1,0:T(8,128)S(1)} %add.303), channel_id=1, source_target_pairs={{0,64},{8,72},{16,80},{24,88},{32,96},{40,104},{48,112},{56,120},{... | collective-permute-start | bytes 1572872 | tf_op jit(solution)/shard_map/ppermute | solution.py:54
  157.7 3.0 copy-start.7
  186.8 297.0 %all-reduce.14.cloned.1.call-start = ((), (), s32[]{:S(2)}) async-start(), calls=%async_computation.2 | async-start | bytes 1048576 | tf_op jit(solution)/shard_map/psum | solution.py:57
  352.8 0.8 copy-start.3
  369.9 113.9 %copy-start.2 = (f32[256,256]{1,0:T(8,128)S(1)}, f32[256,256]{1,0:T(8,128)}, u32[]{:S(2)}) copy-start(f32[256,256]{1,0:T(8,128)} %all-reduce.12.cloned.1.call-done) | copy-start | bytes 786436
  399.1 219.6 %all-reduce.16.cloned.1.call-start = ((), (), s32[]{:S(2)}) async-start(), calls=%async_computation.3 | async-start | bytes 1048576 | tf_op jit(solution)/shard_map/psum | solution.py:57
  533.9 217.8 %all-reduce.18.cloned.1.call-start = ((), (), s32[]{:S(2)}) async-start(), calls=%async_computation.4 | async-start | bytes 1048576 | tf_op jit(solution)/shard_map/psum | solution.py:57
  620.6 1.0 copy-start.5
  621.7 16.1 %copy-start.1 = (bf16[4096,256]{1,0:T(8,128)(2,1)S(1)}, bf16[4096,256]{1,0:T(8,128)(2,1)}, u32[]{:S(2)}) copy-start(bf16[4096,256]{1,0:T(8,128)(2,1)} %copy-done) | copy-start | bytes 6291460
  637.7 115.6 %copy-start.6 = (f32[512,256]{1,0:T(8,128)S(1)}, f32[512,256]{1,0:T(8,128)}, u32[]{:S(2)}) copy-start(f32[512,256]{1,0:T(8,128)} %copy-done.5) | copy-start | bytes 1572868
  666.9 217.6 %all-reduce.20.cloned.1.call-start = ((), (), s32[]{:S(2)}) async-start(), calls=%async_computation.5 | async-start | bytes 1048576 | tf_op jit(solution)/shard_map/psum | solution.py:57
  753.6 0.8 copy-start.4
  799.7 218.8 %all-reduce.22.cloned.1.call-start = ((), (), s32[]{:S(2)}) async-start(), calls=%async_computation.6 | async-start | bytes 1048576 | tf_op jit(solution)/shard_map/psum | solution.py:57
  933.7 217.8 %all-reduce.24.cloned.1.call-start = ((), (), s32[]{:S(2)}) async-start(), calls=%async_computation.7 | async-start | bytes 1048576 | tf_op jit(solution)/shard_map/psum | solution.py:57
  1066.8 217.8 %all-reduce.26.cloned.1.call-start = ((), (), s32[]{:S(2)}) async-start(), calls=%async_computation.8 | async-start | bytes 1048576 | tf_op jit(solution)/shard_map/psum | solution.py:57
Sparse Core Ops, SparseCore 0:
  10.5 34.5 all-gather.2
Sparse Core Ops, SparseCore 1:
  119.3 145.9 all-reduce.11
  268.4 82.6 all-reduce.9
  399.1 84.6 all-reduce.13
  534.0 84.6 all-reduce.15
  667.0 84.6 all-reduce.17
  799.8 84.6 all-reduce.19
  933.8 84.7 all-reduce.21
  1066.8 84.7 all-reduce.23
  1199.8 84.6 all-reduce.25
